TPU v7x, 32 devices: a whole 2x2x4 slice. The times are simulated.
32 devices in a mesh: row: 4 (over y, x), col: 8 (over z, core).
Axes of the slice: x: 2, y: 2, z: 4, core: 2. Of those that a mesh axis runs over, the one named last changes fastest.
Arguments:
- coeffs: bfloat16 [16384, 2048], P('row'), may hold values from -1 to 1
- p_slots: int32 [4, 8, 64], P('row', 'col'), may hold values from 0 to 511, as said below
- p_count: int32 [4, 8], P('row', 'col'), may hold values from 1 to 64
- s_blocks: bfloat16 [4, 8, 64, 128, 128], P('row', 'col'), may hold values from -0.3984375 to 0.3984375
- s_slots: int32 [4, 8, 64], P('row', 'col'), may hold values from 0 to 511, as said below
- s_count: int32 [4, 8], P('row', 'col'), may hold values from 1 to 64
- q_slots: int32 [4, 8, 64], P('row', 'col'), may hold values from 0 to 511, as said below
- q_count: int32 [4, 8], P('row', 'col'), may hold values from 1 to 64
Outputs:
- density: bfloat16 [4, 8, 64, 128, 128], P('row', 'col')
- product: float32 [4, 8, 64, 128, 128], P('row', 'col')
Inputs may be any that keep to these rules, and one draw needn't show every extreme that they name: `p_slots`: on each device the live slots name different blocks of its tile; at least one device has all 64 slots live, which one is drawn. `s_slots`: on each device the live slots name different positions; at least one device has all 64 slots live, which one is drawn. `q_slots`: on each device the live slots name different blocks of its tile; at least one device has all 64 slots live, which one is drawn.
All inputs are finite; a program needn't handle non-finite values.
Results may differ from a plain program's by a relative error of at most 0.0029.
Values may be sent and summed in bfloat16 or wider, within the bound.
No kernel may reach another device: no remote copies, remote signals or barrier semaphores. Data moves between devices by JAX's collectives and lax.ppermute only.
A program may use at most 192 MiB of HBM per device.

v0:
```python
import jax
import jax.numpy as jnp
from jax import lax
from jax.sharding import PartitionSpec as P


def from_root(block, axis, source):
    block = jnp.where(lax.axis_index(axis) == source, block, jnp.zeros_like(block))
    return lax.psum(block, axis)


def shortened(shard):

    def short(part):
        return part.astype(jnp.bfloat16) if part.dtype == jnp.float32 else part

    return jax.tree.map(short, shard)


def shifted(block, axis, distance):
    devices = range(lax.axis_size(axis))
    route = [((i - distance) % len(devices), i) for i in devices]
    return lax.ppermute(block, axis, route)


def step_product(summed, p_data, s_data, panel_slot, q_row, q_col, tile_cols):
    p_blocks, p_code = p_data
    s_blocks, s_code = s_data
    local_k = jnp.arange(tile_cols, dtype=jnp.int32)
    p_live = p_code >= 0
    p_row = jnp.where(p_live, p_code // tile_cols, -1)
    p_col = jnp.where(p_live, p_code % tile_cols, -1)
    pick_left = (
        (p_row[:, None, None] == q_row[None, :, None])
        & (p_col[:, None, None] == local_k[None, None, :])
    ).astype(jnp.bfloat16)
    left_rows = jnp.einsum("pqk,pab->qakb", pick_left, p_blocks, preferred_element_type=jnp.float32)
    left_rows = left_rows.astype(jnp.bfloat16).reshape(q_row.shape[0], 128, tile_cols * 128)
    square = tile_cols * tile_cols
    s_live = (s_code >= 0) & (s_code // square == panel_slot)
    s_local = s_code % square
    s_row = jnp.where(s_live, s_local // tile_cols, -1)
    s_col = s_local % tile_cols
    pick_right = (
        (s_row[:, None, None] == local_k[None, :, None])
        & (s_col[:, None, None] == q_col[None, None, :])
    ).astype(jnp.bfloat16)
    right_cols = jnp.einsum(
        "skq,sab->kaqb", pick_right, s_blocks, preferred_element_type=jnp.float32
    )
    right_cols = right_cols.astype(jnp.bfloat16).reshape(tile_cols * 128, q_row.shape[0], 128)
    return summed + jnp.einsum(
        "qak,kqb->qab", left_rows, right_cols, preferred_element_type=jnp.float32
    )


def pick_tree(flag, moved, kept):
    return jax.tree.map(lambda fresh, stale: jnp.where(flag, fresh, stale), moved, kept)


def on_device(coeffs, p_slots, p_count, s_blocks, s_slots, s_count, q_slots, q_count):
    rows_n = lax.axis_size("row")
    cols_n = lax.axis_size("col")
    row_at = lax.axis_index("row")
    col_at = lax.axis_index("col")
    panel_rows, orbitals = coeffs.shape
    tile_rows = panel_rows // 128
    tile_cols = panel_rows * rows_n // cols_n // 128
    sub_span = cols_n // rows_n
    source = from_root(coeffs, "row", col_at // sub_span)
    column_rows = lax.dynamic_slice_in_dim(
        source, col_at % sub_span * (tile_cols * 128), tile_cols * 128, 0
    )
    slot_ids = p_slots[0, 0]
    p_max = slot_ids.shape[0]
    p_live = jnp.arange(p_max, dtype=jnp.int32) < p_count[0, 0]
    left = coeffs.reshape(tile_rows, 128, orbitals)[slot_ids // tile_cols]
    right = column_rows.reshape(tile_cols, 128, orbitals)[slot_ids % tile_cols]
    raw = jnp.einsum("pak,pbk->pab", left, right, preferred_element_type=jnp.float32)
    dense_blocks = jnp.where(p_live[:, None, None], raw, jnp.zeros_like(raw)).astype(jnp.bfloat16)
    p_code = jnp.where(p_live, slot_ids, -1)
    s_ids = s_slots[0, 0]
    s_max = s_ids.shape[0]
    s_live = jnp.arange(s_max, dtype=jnp.int32) < s_count[0, 0]
    s_code = jnp.where(s_live, s_ids, -1)
    s_local = s_blocks[0, 0]
    q_ids = q_slots[0, 0]
    q_max = q_ids.shape[0]
    q_live = jnp.arange(q_max, dtype=jnp.int32) < q_count[0, 0]
    q_row = q_ids // tile_cols
    q_col = q_ids % tile_cols
    zeros_out = jnp.zeros((q_max, 128, 128), jnp.float32)
    p_data = (dense_blocks, p_code)
    s_data = (s_local, s_code)
    level_count = rows_n.bit_length() - 1
    for level in range(level_count):
        moved = jax.tree.map(
            lambda part, own: part.astype(own.dtype),
            shifted(shortened(p_data), "col", -(1 << level)),
            p_data,
        )
        p_data = pick_tree(row_at >> level & 1 == 1, moved, p_data)
    row_offset = col_at % rows_n
    for level in range(level_count):
        moved = jax.tree.map(
            lambda part, own: part.astype(own.dtype),
            shifted(shortened(s_data), "row", -(1 << level)),
            s_data,
        )
        s_data = pick_tree(row_offset >> level & 1 == 1, moved, s_data)

    def advance(step_at, carry):
        summed, p_held, s_held = carry
        panel_at = (row_at + col_at + step_at) % cols_n
        summed = step_product(summed, p_held, s_held, panel_at // rows_n, q_row, q_col, tile_cols)
        p_held = jax.tree.map(
            lambda part, own: part.astype(own.dtype), shifted(shortened(p_held), "col", -1), p_held
        )
        s_held = jax.tree.map(
            lambda part, own: part.astype(own.dtype), shifted(shortened(s_held), "row", -1), s_held
        )
        return (summed, p_held, s_held)

    summed, p_data, s_data = lax.fori_loop(0, cols_n - 1, advance, (zeros_out, p_data, s_data))
    panel_at = (row_at + col_at + cols_n - 1) % cols_n
    summed = step_product(summed, p_data, s_data, panel_at // rows_n, q_row, q_col, tile_cols)
    product = jnp.where(q_live[:, None, None], summed, jnp.zeros_like(summed))
    return (dense_blocks.reshape(1, 1, p_max, 128, 128), product.reshape(1, 1, q_max, 128, 128))


def solution(mesh):
    return jax.shard_map(
        on_device,
        mesh=mesh,
        in_specs=(
            P("row", None),
            P("row", "col", None),
            P("row", "col"),
            P("row", "col", None, None, None),
            P("row", "col", None),
            P("row", "col"),
            P("row", "col", None),
            P("row", "col"),
        ),
        out_specs=(P("row", "col", None, None, None), P("row", "col", None, None, None)),
        check_vma=False,
    )
```

profile of v0, /device:TPU:0, one launch (start us, length us, event | category | flops | bytes accessed | tf_op | source)
XLA Modules:
  0.0 1880.4 jit_solution(13841358631608636264)
XLA Ops:
  26.0 19.3 %gather_fusion = bf16[64,128,2048]{2,1,0:T(8,128)(2,1)} fusion(bf16[32,128,2048]{2,1,0:T(8,128)(2,1)} %bitcast.130, s32[1024]{0:T(1024)S(1)} %get-tuple-element.386), kind=kCustom, calls=%fused_computation | custom fusion | bytes 67109120 | tf_op jit(solution)/shard_map/gather | solution.py:77
  45.3 329.8 %all-reduce.2.cloned.1.call-done = bf16[4096,2048]{1,0:T(8,128)(2,1)} async-done(((bf16[4096,2048]{1,0:T(8,128)(2,1)}), bf16[4096,2048]{1,0:T(8,128)(2,1)}) %all-reduce.2.cloned.1.call-update) | async-done | bytes 16777232 | tf_op jit(solution)/shard_map/psum | solution.py:9
  383.4 15.9 gather_fusion.1
  399.3 24.5 %select_convert_fusion = bf16[64,128,128]{2,1,0:T(8,128)(2,1)} fusion(pred[64]{0:T(512)(128)(4,1)S(1)} %iota_compare_fusion.5, bf16[64,128,2048]{2,1,0:T(8,128)(2,1)} %gather_fusion, bf16[64,128,2048]{2,1,0:T(8,128)(2,1)} %gather_fusion.1), kind=kOutput, calls=%fused_computation.45 | convolution fusion | flops 4297064448 | bytes 69206080 | tf_op jit(solution)/shard_map/pak,pbk->pab/dot_general | solution.py:79
  431.3 19.0 %collective-permute-done.4 = bf16[64,128,128]{2,1,0:T(8,128)(2,1)} collective-permute-done((bf16[64,128,128]{2,1,0:T(8,128)(2,1)}, bf16[64,128,128]{2,1,0:T(8,128)(2,1)}, u32[]{:S(2)}, u32[]{:S(2)}) %collective-permute-start.4) | collective-permute-done | bytes 2097184 | tf_op jit(solution)/shard_map/ppermute | solution.py:23
  462.1 35.9 %collective-permute-done.6 = s32[64]{0:T(128)S(1)} collective-permute-done((s32[64]{0:T(128)S(1)}, s32[64]{0:T(128)S(1)}, u32[]{:S(2)}, u32[]{:S(2)}) %collective-permute-start.6) | collective-permute-done | bytes 288 | tf_op jit(solution)/shard_map/ppermute | solution.py:23
  508.6 1178.4 %while.25 = (s32[]{:T(128)}, f32[64,128,128]{2,1,0:T(8,128)}, bf16[64,128,128]{2,0,1:T(8,128)(2,1)}, s32[64]{0:T(128)S(1)}, bf16[64,128,128]{2,0,1:T(8,128)(2,1)...) while((s32[]{:T(128)}, f32[64,128,128]{2,1,0:T(8,128)}, ...), condition=%wide.region_2.3_spmd.clone, body=%wide.region_1.2_spmd.clone.sunk | while | flops 8625731584 | bytes 239103024 | solution.py:124
  536.0 49.3 %reshape.448 = bf16[64,128,2048]{2,1,0:T(8,128)(2,1)} reshape(bf16[64,128,16,128]{3,2,1,0:T(8,128)(2,1)} %convert_bitcast_fusion.4) | data formatting | bytes 67108864 | tf_op jit(solution)/shard_map/while/body/eval_jaxpr/reshape | solution.py:38
  600.8 79.3 %select_add_fusion.2 = f32[64,128,128]{2,1,0:T(8,128)} fusion(f32[64,128,128]{2,1,0:T(8,128)} %get-tuple-element.471, pred[]{:T(512)S(6)} %compare.95, bf16[64,128,2048]{2,1,0:T(8,128)(2,1)} %reshape.448, bf16[2048,64,128]{2,1,0:T(8,128)(2,1)} %bitcast.128), kind=kOutput, calls=%fused_computation.6.clone.1 | convolution fusion | flops 4297064448 | bytes 75497472 | tf_op jit(solution)/shard_map/while/body/eval_jaxpr/qak,kqb->qab/dot_general | solution.py:52
  700.7 49.3 %reshape.448 = bf16[64,128,2048]{2,1,0:T(8,128)(2,1)} reshape(bf16[64,128,16,128]{3,2,1,0:T(8,128)(2,1)} %convert_bitcast_fusion.4) | data formatting | bytes 67108864 | tf_op jit(solution)/shard_map/while/body/eval_jaxpr/reshape | solution.py:38
  765.6 80.5 %select_add_fusion.2 = f32[64,128,128]{2,1,0:T(8,128)} fusion(f32[64,128,128]{2,1,0:T(8,128)} %get-tuple-element.471, pred[]{:T(512)S(6)} %compare.95, bf16[64,128,2048]{2,1,0:T(8,128)(2,1)} %reshape.448, bf16[2048,64,128]{2,1,0:T(8,128)(2,1)} %bitcast.128), kind=kOutput, calls=%fused_computation.6.clone.1 | convolution fusion | flops 4297064448 | bytes 75497472 | tf_op jit(solution)/shard_map/while/body/eval_jaxpr/qak,kqb->qab/dot_general | solution.py:52
  869.5 49.3 %reshape.448 = bf16[64,128,2048]{2,1,0:T(8,128)(2,1)} reshape(bf16[64,128,16,128]{3,2,1,0:T(8,128)(2,1)} %convert_bitcast_fusion.4) | data formatting | bytes 67108864 | tf_op jit(solution)/shard_map/while/body/eval_jaxpr/reshape | solution.py:38
  934.3 80.5 %select_add_fusion.2 = f32[64,128,128]{2,1,0:T(8,128)} fusion(f32[64,128,128]{2,1,0:T(8,128)} %get-tuple-element.471, pred[]{:T(512)S(6)} %compare.95, bf16[64,128,2048]{2,1,0:T(8,128)(2,1)} %reshape.448, bf16[2048,64,128]{2,1,0:T(8,128)(2,1)} %bitcast.128), kind=kOutput, calls=%fused_computation.6.clone.1 | convolution fusion | flops 4297064448 | bytes 75497472 | tf_op jit(solution)/shard_map/while/body/eval_jaxpr/qak,kqb->qab/dot_general | solution.py:52
  1035.6 49.3 %reshape.448 = bf16[64,128,2048]{2,1,0:T(8,128)(2,1)} reshape(bf16[64,128,16,128]{3,2,1,0:T(8,128)(2,1)} %convert_bitcast_fusion.4) | data formatting | bytes 67108864 | tf_op jit(solution)/shard_map/while/body/eval_jaxpr/reshape | solution.py:38
  1100.4 80.5 %select_add_fusion.2 = f32[64,128,128]{2,1,0:T(8,128)} fusion(f32[64,128,128]{2,1,0:T(8,128)} %get-tuple-element.471, pred[]{:T(512)S(6)} %compare.95, bf16[64,128,2048]{2,1,0:T(8,128)(2,1)} %reshape.448, bf16[2048,64,128]{2,1,0:T(8,128)(2,1)} %bitcast.128), kind=kOutput, calls=%fused_computation.6.clone.1 | convolution fusion | flops 4297064448 | bytes 75497472 | tf_op jit(solution)/shard_map/while/body/eval_jaxpr/qak,kqb->qab/dot_general | solution.py:52
  1206.6 49.3 %reshape.448 = bf16[64,128,2048]{2,1,0:T(8,128)(2,1)} reshape(bf16[64,128,16,128]{3,2,1,0:T(8,128)(2,1)} %convert_bitcast_fusion.4) | data formatting | bytes 67108864 | tf_op jit(solution)/shard_map/while/body/eval_jaxpr/reshape | solution.py:38
  1271.4 80.5 %select_add_fusion.2 = f32[64,128,128]{2,1,0:T(8,128)} fusion(f32[64,128,128]{2,1,0:T(8,128)} %get-tuple-element.471, pred[]{:T(512)S(6)} %compare.95, bf16[64,128,2048]{2,1,0:T(8,128)(2,1)} %reshape.448, bf16[2048,64,128]{2,1,0:T(8,128)(2,1)} %bitcast.128), kind=kOutput, calls=%fused_computation.6.clone.1 | convolution fusion | flops 4297064448 | bytes 75497472 | tf_op jit(solution)/shard_map/while/body/eval_jaxpr/qak,kqb->qab/dot_general | solution.py:52
  1372.6 49.3 %reshape.448 = bf16[64,128,2048]{2,1,0:T(8,128)(2,1)} reshape(bf16[64,128,16,128]{3,2,1,0:T(8,128)(2,1)} %convert_bitcast_fusion.4) | data formatting | bytes 67108864 | tf_op jit(solution)/shard_map/while/body/eval_jaxpr/reshape | solution.py:38
  1437.4 80.5 %select_add_fusion.2 = f32[64,128,128]{2,1,0:T(8,128)} fusion(f32[64,128,128]{2,1,0:T(8,128)} %get-tuple-element.471, pred[]{:T(512)S(6)} %compare.95, bf16[64,128,2048]{2,1,0:T(8,128)(2,1)} %reshape.448, bf16[2048,64,128]{2,1,0:T(8,128)(2,1)} %bitcast.128), kind=kOutput, calls=%fused_computation.6.clone.1 | convolution fusion | flops 4297064448 | bytes 75497472 | tf_op jit(solution)/shard_map/while/body/eval_jaxpr/qak,kqb->qab/dot_general | solution.py:52
  1541.3 49.3 %reshape.448 = bf16[64,128,2048]{2,1,0:T(8,128)(2,1)} reshape(bf16[64,128,16,128]{3,2,1,0:T(8,128)(2,1)} %convert_bitcast_fusion.4) | data formatting | bytes 67108864 | tf_op jit(solution)/shard_map/while/body/eval_jaxpr/reshape | solution.py:38
  1606.1 80.5 %select_add_fusion.2 = f32[64,128,128]{2,1,0:T(8,128)} fusion(f32[64,128,128]{2,1,0:T(8,128)} %get-tuple-element.471, pred[]{:T(512)S(6)} %compare.95, bf16[64,128,2048]{2,1,0:T(8,128)(2,1)} %reshape.448, bf16[2048,64,128]{2,1,0:T(8,128)(2,1)} %bitcast.128), kind=kOutput, calls=%fused_computation.6.clone.1 | convolution fusion | flops 4297064448 | bytes 75497472 | tf_op jit(solution)/shard_map/while/body/eval_jaxpr/qak,kqb->qab/dot_general | solution.py:52
  1702.7 47.4 %copy.16 = bf16[64,128,16,128]{1,3,2,0:T(8,128)(2,1)} copy(bf16[64,128,16,128]{3,0,2,1:T(8,128)(2,1)} %convert_bitcast_fusion.2) | data formatting | bytes 67108864 | tf_op jit(solution)/shard_map/convert_element_type | solution.py:38
  1765.9 23.1 %copy.17 = bf16[16,128,64,128]{3,2,1,0:T(8,128)(2,1)} copy(bf16[16,128,64,128]{3,2,0,1:T(8,128)(2,1)} %convert_bitcast_fusion.1) | data formatting | bytes 67108864 | tf_op jit(solution)/shard_map/convert_element_type | solution.py:51
  1789.0 78.4 %fusion.14 = f32[64,128,128]{2,1,0:T(8,128)} fusion(bf16[64,128,2048]{1,2,0:T(8,128)(2,1)} %bitcast.131, bf16[2048,64,128]{2,1,0:T(8,128)(2,1)} %bitcast.132), kind=kOutput, calls=%fused_computation.39 | convolution fusion | flops 4294967296 | bytes 71303168 | tf_op jit(solution)/shard_map/qak,kqb->qab/dot_general | solution.py:52
  (199 shorter events, 362.1 us)
Async XLA Ops:
  7.2 367.9 %all-reduce.2.cloned.1.call-start = ((), (), s32[]{:S(2)}) async-start(), calls=%async_computation | async-start | bytes 33554432 | tf_op jit(solution)/shard_map/psum | solution.py:9
  25.3 401.2 %collective-permute-start.8 = (bf16[64,128,128]{2,0,1:T(8,128)(2,1)}, bf16[64,128,128]{2,0,1:T(8,128)(2,1)}, u32[]{:S(2)}, u32[]{:S(2)}) collective-permute-start(bf16[64,128,128]{2,0,1:T(8,128)(2,1)} %bitcast.107), channel_id=1, source_target_pairs={{8,0},{16,8},{24,16},{0,24},{9,1},{17,9},{25,17},{1,25},{10,2},{18... | collective-permute-start | bytes 6291464 | tf_op jit(solution)/shard_map/ppermute | solution.py:23
  510.4 169.7 %collective-permute-start = (bf16[64,128,128]{2,0,1:T(8,128)(2,1)S(1)}, bf16[64,128,128]{2,0,1:T(8,128)(2,1)}, u32[]{:S(2)}, u32[]{:S(2)}) collective-permute-start(bf16[64,128,128]{2,0,1:T(8,128)(2,1)S(1)} %copy.46), channel_id=1, source_target_pairs={{1,0},{2,1},{3,2},{4,3},{5,4},{6,5},{7,6},{0,7},{9,8},{10,9},{11,1... | collective-permute-start | bytes 6291464 | tf_op jit(solution)/shard_map/while/body/eval_jaxpr/ppermute | solution.py:23
  515.6 164.5 %collective-permute-start.1 = (s32[64]{0:T(128)S(1)}, s32[64]{0:T(128)S(1)}, u32[]{:S(2)}, u32[]{:S(2)}) collective-permute-start(s32[64]{0:T(128)S(1)} %copy.47), channel_id=1, source_target_pairs={{1,0},{2,1},{3,2},{4,3},{5,4},{6,5},{7,6},{0,7},{9,8},{10,9},{11,1... | collective-permute-start | bytes 776 | tf_op jit(solution)/shard_map/while/body/eval_jaxpr/ppermute | solution.py:23
  518.8 161.3 %collective-permute-start.2 = (bf16[64,128,128]{2,0,1:T(8,128)(2,1)}, bf16[64,128,128]{2,0,1:T(8,128)(2,1)}, u32[]{:S(2)}, u32[]{:S(2)}) collective-permute-start(bf16[64,128,128]{2,0,1:T(8,128)(2,1)} %copy.48), channel_id=1, source_target_pairs={{8,0},{16,8},{24,16},{0,24},{9,1},{17,9},{25,17},{1,25},{10,2},{18... | collective-permute-start | bytes 6291464 | tf_op jit(solution)/shard_map/while/body/eval_jaxpr/ppermute | solution.py:23
  681.7 164.3 %collective-permute-start = (bf16[64,128,128]{2,0,1:T(8,128)(2,1)S(1)}, bf16[64,128,128]{2,0,1:T(8,128)(2,1)}, u32[]{:S(2)}, u32[]{:S(2)}) collective-permute-start(bf16[64,128,128]{2,0,1:T(8,128)(2,1)S(1)} %copy.46), channel_id=1, source_target_pairs={{1,0},{2,1},{3,2},{4,3},{5,4},{6,5},{7,6},{0,7},{9,8},{10,9},{11,1... | collective-permute-start | bytes 6291464 | tf_op jit(solution)/shard_map/while/body/eval_jaxpr/ppermute | solution.py:23
  681.7 164.3 %collective-permute-start.1 = (s32[64]{0:T(128)S(1)}, s32[64]{0:T(128)S(1)}, u32[]{:S(2)}, u32[]{:S(2)}) collective-permute-start(s32[64]{0:T(128)S(1)} %copy.47), channel_id=1, source_target_pairs={{1,0},{2,1},{3,2},{4,3},{5,4},{6,5},{7,6},{0,7},{9,8},{10,9},{11,1... | collective-permute-start | bytes 776 | tf_op jit(solution)/shard_map/while/body/eval_jaxpr/ppermute | solution.py:23
  684.9 161.2 %collective-permute-start.2 = (bf16[64,128,128]{2,0,1:T(8,128)(2,1)}, bf16[64,128,128]{2,0,1:T(8,128)(2,1)}, u32[]{:S(2)}, u32[]{:S(2)}) collective-permute-start(bf16[64,128,128]{2,0,1:T(8,128)(2,1)} %copy.48), channel_id=1, source_target_pairs={{8,0},{16,8},{24,16},{0,24},{9,1},{17,9},{25,17},{1,25},{10,2},{18... | collective-permute-start | bytes 6291464 | tf_op jit(solution)/shard_map/while/body/eval_jaxpr/ppermute | solution.py:23
  847.7 167.1 %collective-permute-start = (bf16[64,128,128]{2,0,1:T(8,128)(2,1)S(1)}, bf16[64,128,128]{2,0,1:T(8,128)(2,1)}, u32[]{:S(2)}, u32[]{:S(2)}) collective-permute-start(bf16[64,128,128]{2,0,1:T(8,128)(2,1)S(1)} %copy.46), channel_id=1, source_target_pairs={{1,0},{2,1},{3,2},{4,3},{5,4},{6,5},{7,6},{0,7},{9,8},{10,9},{11,1... | collective-permute-start | bytes 6291464 | tf_op jit(solution)/shard_map/while/body/eval_jaxpr/ppermute | solution.py:23
  848.1 166.7 %collective-permute-start.1 = (s32[64]{0:T(128)S(1)}, s32[64]{0:T(128)S(1)}, u32[]{:S(2)}, u32[]{:S(2)}) collective-permute-start(s32[64]{0:T(128)S(1)} %copy.47), channel_id=1, source_target_pairs={{1,0},{2,1},{3,2},{4,3},{5,4},{6,5},{7,6},{0,7},{9,8},{10,9},{11,1... | collective-permute-start | bytes 776 | tf_op jit(solution)/shard_map/while/body/eval_jaxpr/ppermute | solution.py:23
  852.4 162.4 %collective-permute-start.2 = (bf16[64,128,128]{2,0,1:T(8,128)(2,1)}, bf16[64,128,128]{2,0,1:T(8,128)(2,1)}, u32[]{:S(2)}, u32[]{:S(2)}) collective-permute-start(bf16[64,128,128]{2,0,1:T(8,128)(2,1)} %copy.48), channel_id=1, source_target_pairs={{8,0},{16,8},{24,16},{0,24},{9,1},{17,9},{25,17},{1,25},{10,2},{18... | collective-permute-start | bytes 6291464 | tf_op jit(solution)/shard_map/while/body/eval_jaxpr/ppermute | solution.py:23
  854.9 159.9 %collective-permute-start.3 = (s32[64]{0:T(128)S(1)}, s32[64]{0:T(128)S(1)}, u32[]{:S(2)}, u32[]{:S(2)}) collective-permute-start(s32[64]{0:T(128)S(1)} %copy.49), channel_id=1, source_target_pairs={{8,0},{16,8},{24,16},{0,24},{9,1},{17,9},{25,17},{1,25},{10,2},{18... | collective-permute-start | bytes 776 | tf_op jit(solution)/shard_map/while/body/eval_jaxpr/ppermute | solution.py:23
  1016.4 164.5 %collective-permute-start = (bf16[64,128,128]{2,0,1:T(8,128)(2,1)S(1)}, bf16[64,128,128]{2,0,1:T(8,128)(2,1)}, u32[]{:S(2)}, u32[]{:S(2)}) collective-permute-start(bf16[64,128,128]{2,0,1:T(8,128)(2,1)S(1)} %copy.46), channel_id=1, source_target_pairs={{1,0},{2,1},{3,2},{4,3},{5,4},{6,5},{7,6},{0,7},{9,8},{10,9},{11,1... | collective-permute-start | bytes 6291464 | tf_op jit(solution)/shard_map/while/body/eval_jaxpr/ppermute | solution.py:23
  1016.4 164.5 %collective-permute-start.1 = (s32[64]{0:T(128)S(1)}, s32[64]{0:T(128)S(1)}, u32[]{:S(2)}, u32[]{:S(2)}) collective-permute-start(s32[64]{0:T(128)S(1)} %copy.47), channel_id=1, source_target_pairs={{1,0},{2,1},{3,2},{4,3},{5,4},{6,5},{7,6},{0,7},{9,8},{10,9},{11,1... | collective-permute-start | bytes 776 | tf_op jit(solution)/shard_map/while/body/eval_jaxpr/ppermute | solution.py:23
  1019.7 161.2 %collective-permute-start.2 = (bf16[64,128,128]{2,0,1:T(8,128)(2,1)}, bf16[64,128,128]{2,0,1:T(8,128)(2,1)}, u32[]{:S(2)}, u32[]{:S(2)}) collective-permute-start(bf16[64,128,128]{2,0,1:T(8,128)(2,1)} %copy.48), channel_id=1, source_target_pairs={{8,0},{16,8},{24,16},{0,24},{9,1},{17,9},{25,17},{1,25},{10,2},{18... | collective-permute-start | bytes 6291464 | tf_op jit(solution)/shard_map/while/body/eval_jaxpr/ppermute | solution.py:23
  1182.5 169.4 %collective-permute-start = (bf16[64,128,128]{2,0,1:T(8,128)(2,1)S(1)}, bf16[64,128,128]{2,0,1:T(8,128)(2,1)}, u32[]{:S(2)}, u32[]{:S(2)}) collective-permute-start(bf16[64,128,128]{2,0,1:T(8,128)(2,1)S(1)} %copy.46), channel_id=1, source_target_pairs={{1,0},{2,1},{3,2},{4,3},{5,4},{6,5},{7,6},{0,7},{9,8},{10,9},{11,1... | collective-permute-start | bytes 6291464 | tf_op jit(solution)/shard_map/while/body/eval_jaxpr/ppermute | solution.py:23
  1184.0 167.9 %collective-permute-start.1 = (s32[64]{0:T(128)S(1)}, s32[64]{0:T(128)S(1)}, u32[]{:S(2)}, u32[]{:S(2)}) collective-permute-start(s32[64]{0:T(128)S(1)} %copy.47), channel_id=1, source_target_pairs={{1,0},{2,1},{3,2},{4,3},{5,4},{6,5},{7,6},{0,7},{9,8},{10,9},{11,1... | collective-permute-start | bytes 776 | tf_op jit(solution)/shard_map/while/body/eval_jaxpr/ppermute | solution.py:23
  1189.4 162.5 %collective-permute-start.2 = (bf16[64,128,128]{2,0,1:T(8,128)(2,1)}, bf16[64,128,128]{2,0,1:T(8,128)(2,1)}, u32[]{:S(2)}, u32[]{:S(2)}) collective-permute-start(bf16[64,128,128]{2,0,1:T(8,128)(2,1)} %copy.48), channel_id=1, source_target_pairs={{8,0},{16,8},{24,16},{0,24},{9,1},{17,9},{25,17},{1,25},{10,2},{18... | collective-permute-start | bytes 6291464 | tf_op jit(solution)/shard_map/while/body/eval_jaxpr/ppermute | solution.py:23
  1353.6 164.3 %collective-permute-start = (bf16[64,128,128]{2,0,1:T(8,128)(2,1)S(1)}, bf16[64,128,128]{2,0,1:T(8,128)(2,1)}, u32[]{:S(2)}, u32[]{:S(2)}) collective-permute-start(bf16[64,128,128]{2,0,1:T(8,128)(2,1)S(1)} %copy.46), channel_id=1, source_target_pairs={{1,0},{2,1},{3,2},{4,3},{5,4},{6,5},{7,6},{0,7},{9,8},{10,9},{11,1... | collective-permute-start | bytes 6291464 | tf_op jit(solution)/shard_map/while/body/eval_jaxpr/ppermute | solution.py:23
  1353.6 164.3 %collective-permute-start.1 = (s32[64]{0:T(128)S(1)}, s32[64]{0:T(128)S(1)}, u32[]{:S(2)}, u32[]{:S(2)}) collective-permute-start(s32[64]{0:T(128)S(1)} %copy.47), channel_id=1, source_target_pairs={{1,0},{2,1},{3,2},{4,3},{5,4},{6,5},{7,6},{0,7},{9,8},{10,9},{11,1... | collective-permute-start | bytes 776 | tf_op jit(solution)/shard_map/while/body/eval_jaxpr/ppermute | solution.py:23
  1356.7 161.2 %collective-permute-start.2 = (bf16[64,128,128]{2,0,1:T(8,128)(2,1)}, bf16[64,128,128]{2,0,1:T(8,128)(2,1)}, u32[]{:S(2)}, u32[]{:S(2)}) collective-permute-start(bf16[64,128,128]{2,0,1:T(8,128)(2,1)} %copy.48), channel_id=1, source_target_pairs={{8,0},{16,8},{24,16},{0,24},{9,1},{17,9},{25,17},{1,25},{10,2},{18... | collective-permute-start | bytes 6291464 | tf_op jit(solution)/shard_map/while/body/eval_jaxpr/ppermute | solution.py:23
  1519.5 167.1 %collective-permute-start = (bf16[64,128,128]{2,0,1:T(8,128)(2,1)S(1)}, bf16[64,128,128]{2,0,1:T(8,128)(2,1)}, u32[]{:S(2)}, u32[]{:S(2)}) collective-permute-start(bf16[64,128,128]{2,0,1:T(8,128)(2,1)S(1)} %copy.46), channel_id=1, source_target_pairs={{1,0},{2,1},{3,2},{4,3},{5,4},{6,5},{7,6},{0,7},{9,8},{10,9},{11,1... | collective-permute-start | bytes 6291464 | tf_op jit(solution)/shard_map/while/body/eval_jaxpr/ppermute | solution.py:23
  1519.5 167.1 %collective-permute-start.1 = (s32[64]{0:T(128)S(1)}, s32[64]{0:T(128)S(1)}, u32[]{:S(2)}, u32[]{:S(2)}) collective-permute-start(s32[64]{0:T(128)S(1)} %copy.47), channel_id=1, source_target_pairs={{1,0},{2,1},{3,2},{4,3},{5,4},{6,5},{7,6},{0,7},{9,8},{10,9},{11,1... | collective-permute-start | bytes 776 | tf_op jit(solution)/shard_map/while/body/eval_jaxpr/ppermute | solution.py:23
  1524.2 162.4 %collective-permute-start.2 = (bf16[64,128,128]{2,0,1:T(8,128)(2,1)}, bf16[64,128,128]{2,0,1:T(8,128)(2,1)}, u32[]{:S(2)}, u32[]{:S(2)}) collective-permute-start(bf16[64,128,128]{2,0,1:T(8,128)(2,1)} %copy.48), channel_id=1, source_target_pairs={{8,0},{16,8},{24,16},{0,24},{9,1},{17,9},{25,17},{1,25},{10,2},{18... | collective-permute-start | bytes 6291464 | tf_op jit(solution)/shard_map/while/body/eval_jaxpr/ppermute | solution.py:23
  (19 other events, 1391.4 us)
Sparse Core Ops, SparseCore 0:
  21.1 353.9 all-reduce.1
where the time goes:
time: 1900 us; the launch traced here: 1880 us
  matrix products  902 us (47%)
  local copies, waits for them, and re-layouts  499 us (26%)
  waiting for transfers between devices  387 us (20%)
  starting transfers between devices  43.3 us (2%)
  other arithmetic  31.6 us (2%)
    dot_general x8, matrix products, step_product(): jnp.einsum('qak,kqb->qab', left_rows, right_cols, preferred_element_type=...  641 us
    reshape x7, local copies, waits for them, and re-layouts, step_product(): left_rows.astype(jnp.bfloat16).reshape(q_row.shape[0], 128, tile_cols * 128)  345 us
    psum x1, waiting for transfers between devices, from_root(): return lax.psum(block, axis)  330 us
    dot_general x8, matrix products, step_product(): jnp.einsum('skq,sab->kaqb', pick_right, s_blocks, preferred_element_type=...  124 us
    dot_general x8, matrix products, step_product(): jnp.einsum('pqk,pab->qakb', pick_left, p_blocks, preferred_element_type=j...  112 us
    ppermute x36, waiting for transfers between devices, shifted(): return lax.ppermute(block, axis, route)  57 us
    convert_element_type x1, local copies, waits for them, and re-layouts, step_product(): left_rows.astype(jnp.bfloat16).reshape(q_row.shape[0], 128, tile_cols * 128)  47.4 us
    ppermute x36, starting transfers between devices, shifted(): return lax.ppermute(block, axis, route)  43.3 us
  transfers between devices with their start and end apart: 37, of which 5 were waited for; matrix products, arithmetic and copies ran while one was open for 65% of the time, Pallas kernels for 0%

commit v1 on v0

v1 whole, which is shorter than its diff:
```python
import jax
import jax.numpy as jnp
from jax import lax
from jax.experimental import pallas as pl
from jax.experimental.pallas import tpu as pltpu
from jax.sharding import PartitionSpec as P

VMEM_LIMIT = 58 * 1024 * 1024


def density_kernel(count_ref, row_ref, col_ref, left_ref, right_ref, out_ref):
    count = count_ref[0]

    def compute(slot, carry):
        out_ref[slot] = lax.dot_general(
            left_ref[row_ref[slot]],
            right_ref[col_ref[slot]],
            (((1,), (1,)), ((), ())),
            preferred_element_type=jnp.float32,
        ).astype(out_ref.dtype)
        return carry

    def clear(slot, carry):
        out_ref[slot] = jnp.zeros(out_ref.shape[1:], out_ref.dtype)
        return carry

    lax.fori_loop(0, count, compute, 0)
    lax.fori_loop(count, out_ref.shape[0], clear, 0)


def density_blocks(count, rows, cols, left, right):
    smem = pl.BlockSpec(memory_space=pltpu.SMEM)
    vmem = pl.BlockSpec(memory_space=pltpu.VMEM)
    return pl.pallas_call(
        density_kernel,
        out_shape=jax.ShapeDtypeStruct((rows.shape[0], 128, 128), jnp.bfloat16),
        in_specs=[smem, smem, smem, vmem, vmem],
        out_specs=vmem,
        compiler_params=pltpu.CompilerParams(vmem_limit_bytes=VMEM_LIMIT),
        name="density_blocks",
    )(count, rows, cols, left, right)


EAGER = 2


def product_kernel(count_ref, left_at, right_at, p_hbm, *rest):
    parts = len(rest) - 4
    s_hbm = rest[:parts]
    out_ref, p_ref, s_ref, sems = rest[parts:]
    s_max = s_ref.shape[0] // parts
    copies = [pltpu.make_async_copy(p_hbm, p_ref, sems.at[parts])]
    for d in range(parts):
        copies.append(
            pltpu.make_async_copy(s_hbm[d], s_ref.at[pl.ds(d * s_max, s_max)], sems.at[d])
        )
    for copy in copies:
        copy.start()
    for copy in copies:
        copy.wait()

    def pair(q, n):
        return jnp.dot(
            p_ref[left_at[q, n]], s_ref[right_at[q, n]], preferred_element_type=jnp.float32
        )

    def eager(q, carry):
        count = count_ref[q]
        total = jnp.zeros(out_ref.shape[1:], jnp.float32)
        for n in range(EAGER):
            total = total + jnp.where(n < count, pair(q, n), 0.0)
        out_ref[q] = total
        return carry

    def rest_of(q, carry):
        def add(n, inner):
            out_ref[q] += pair(q, n)
            return inner

        return lax.fori_loop(EAGER, count_ref[q], add, carry)

    lax.fori_loop(0, out_ref.shape[0], eager, 0, unroll=4)
    lax.fori_loop(0, out_ref.shape[0], rest_of, 0)


def product_blocks(counts, left_at, right_at, p_all, s_parts):
    smem = pl.BlockSpec(memory_space=pltpu.SMEM)
    hbm = pl.BlockSpec(memory_space=pl.ANY)
    parts = len(s_parts)
    s_max = s_parts[0].shape[0]
    return pl.pallas_call(
        product_kernel,
        out_shape=jax.ShapeDtypeStruct((counts.shape[0], 128, 128), jnp.float32),
        in_specs=[smem, smem, smem, hbm] + [hbm] * parts,
        out_specs=pl.BlockSpec(memory_space=pltpu.VMEM),
        scratch_shapes=[
            pltpu.VMEM(p_all.shape, p_all.dtype),
            pltpu.VMEM((parts * s_max, 128, 128), s_parts[0].dtype),
            pltpu.SemaphoreType.DMA((parts + 1,)),
        ],
        compiler_params=pltpu.CompilerParams(vmem_limit_bytes=VMEM_LIMIT),
        name="product_blocks",
    )(counts, left_at, right_at, p_all, *s_parts)


def exact_dot(left, right):
    return jnp.dot(
        left.astype(jnp.float32),
        right.astype(jnp.float32),
        precision=lax.Precision.HIGHEST,
        preferred_element_type=jnp.float32,
    )


def found_at(mine, theirs, live, place, inner, inner_count):
    hit = (mine[:, None] == theirs[None, :]) & live[None, :]
    weight = jnp.where(hit, place[None, :] + 1, 0)
    at = inner[:, None] == jnp.arange(inner_count, dtype=jnp.int32)[None, :]
    return exact_dot(weight, at)


def on_device(coeffs, p_slots, p_count, s_blocks, s_slots, s_count, q_slots, q_count):
    rows_n = lax.axis_size("row")
    cols_n = lax.axis_size("col")
    row_at = lax.axis_index("row")
    col_at = lax.axis_index("col")
    panel_rows, orbitals = coeffs.shape
    tile_rows = panel_rows // 128
    tile_cols = panel_rows * rows_n // cols_n // 128
    span = cols_n // rows_n
    k_count = cols_n * tile_cols

    piece = tile_cols * 128 // rows_n
    start = col_at % span * (tile_cols * 128) + col_at // span * piece
    route = []
    for r in range(rows_n):
        for c in range(cols_n):
            to = (c // span) * cols_n + r * span + c % span
            route.append((r * cols_n + c, to))
    sent = lax.dynamic_slice_in_dim(coeffs, start, piece, 0)
    got = lax.ppermute(sent, ("row", "col"), route)
    column_rows = lax.all_gather(got, "row", axis=0, tiled=True)

    p_ids = p_slots[0, 0]
    p_max = p_ids.shape[0]
    p_code = jnp.where(jnp.arange(p_max, dtype=jnp.int32) < p_count[0, 0], p_ids, -1)
    s_ids = s_slots[0, 0]
    s_max = s_ids.shape[0]
    s_code = jnp.where(jnp.arange(s_max, dtype=jnp.int32) < s_count[0, 0], s_ids, -1)
    q_ids = q_slots[0, 0]
    q_max = q_ids.shape[0]
    q_live = jnp.arange(q_max, dtype=jnp.int32) < q_count[0, 0]
    q_row = q_ids // tile_cols
    q_col = q_ids % tile_cols

    p_codes = lax.all_gather(p_code, "col").reshape(-1)
    s_codes = lax.all_gather(s_code, "row").reshape(-1)
    p_place = jnp.arange(cols_n * p_max, dtype=jnp.int32)
    p_live = p_codes >= 0
    p_local = jnp.maximum(p_codes, 0)
    p_k = p_place // p_max * tile_cols + p_local % tile_cols
    p_found = found_at(q_row, p_local // tile_cols, p_live, p_place, p_k, k_count)
    s_order = jnp.arange(rows_n * s_max, dtype=jnp.int32)
    s_from = s_order // s_max
    s_place = (row_at - s_from + rows_n) % rows_n * s_max + s_order % s_max
    s_live = s_codes >= 0
    s_local = jnp.maximum(s_codes, 0)
    local_row = s_local // tile_cols
    s_k = (s_from + rows_n * (local_row // tile_cols)) * tile_cols + local_row % tile_cols
    s_found = found_at(q_col, s_local % tile_cols, s_live, s_place, s_k, k_count)
    match = (p_found > 0) & (s_found > 0) & q_live[:, None]
    steps = jnp.arange(k_count, dtype=jnp.int32)
    rank = exact_dot(match, steps[:, None] < steps[None, :]).astype(jnp.int32)
    code = (p_found.astype(jnp.int32) - 1) * (rows_n * s_max) + s_found.astype(jnp.int32) - 1
    chosen = match[:, None, :] & (rank[:, None, :] == steps[None, :, None])
    listed = jnp.sum(jnp.where(chosen, code[:, None, :], 0), axis=2, dtype=jnp.int32)
    counts = jnp.sum(match, axis=1, dtype=jnp.int32)
    left_at = listed // (rows_n * s_max)
    right_at = listed % (rows_n * s_max)

    dense = density_blocks(
        p_count[0],
        p_ids // tile_cols,
        p_ids % tile_cols,
        coeffs.reshape(tile_rows, 128, orbitals),
        column_rows.reshape(tile_cols, 128, orbitals),
    )
    p_all = lax.all_gather(dense, "col", axis=0, tiled=True)
    s_own, _ = lax.optimization_barrier((s_blocks[0, 0], dense))
    s_parts = [s_own]
    for d in range(1, rows_n):
        s_parts.append(lax.ppermute(s_own, "row", [(i, (i + d) % rows_n) for i in range(rows_n)]))
    product = product_blocks(counts, left_at, right_at, p_all, s_parts)
    return (dense.reshape(1, 1, p_max, 128, 128), product.reshape(1, 1, q_max, 128, 128))


def solution(mesh):
    return jax.shard_map(
        on_device,
        mesh=mesh,
        in_specs=(
            P("row", None),
            P("row", "col", None),
            P("row", "col"),
            P("row", "col", None, None, None),
            P("row", "col", None),
            P("row", "col"),
            P("row", "col", None),
            P("row", "col"),
        ),
        out_specs=(P("row", "col", None, None, None), P("row", "col", None, None, None)),
        check_vma=False,
    )
```

time: 1900 us -> 442 us (0.23); the launches traced: 1880 us -> 441 us
  matrix products: 902 us -> 1.43 us
  local copies, waits for them, and re-layouts: 499 us -> 3.71 us
  starting transfers between devices: 43.3 us -> 3.3 us
  waiting for transfers between devices: 387 us -> 351 us
  Pallas kernels: 0 us -> 34.4 us
  blocking collectives: 0 us -> 29.1 us
  other arithmetic: 31.6 us -> 2.66 us
    dot_general x25 -> x3, matrix products: 902 us -> 1.43 us  [exact_dot(): jnp.dot(left.astype(jnp.float32), right.astype(jnp.float32), precision=la...]
    reshape x7 -> x0, local copies, waits for them, and re-layouts: 345 us -> none  [step_product(): left_rows.astype(jnp.bfloat16).reshape(q_row.shape[0], 128, tile_cols * 128)]
    psum x1 -> x0, waiting for transfers between devices: 330 us -> none  [from_root(): return lax.psum(block, axis)]
    all_gather x0 -> x2, waiting for transfers between devices: none -> 264 us  [the longest x1 227 us: on_device(): column_rows = lax.all_gather(got, 'row', axis=0, tiled=True)]
    convert_element_type x2 -> x0, local copies, waits for them, and re-layouts: 70.6 us -> none  [the longest x1 47.4 us: step_product(): left_rows.astype(jnp.bfloat16).reshape(q_row.shape[0], 128, tile_cols * 128)]
    ppermute x36 -> x4, starting transfers between devices: 43.3 us -> 3.22 us  [the longest x3 2.43 us: on_device(): lax.ppermute(s_own, 'row', [(i, (i + d) % rows_n) for i in range(rows_n)])]
    gather x2 -> x0, local copies, waits for them, and re-layouts: 35.2 us -> none  [the longest x1 19.3 us: on_device(): left = coeffs.reshape(tile_rows, 128, orbitals)[slot_ids // tile_cols]]
    pallas_call x0 -> x2, Pallas kernels: none -> 34.4 us  [the longest x1 18 us: density_blocks(): pl.pallas_call(density_kernel, out_shape=jax.ShapeDtypeStruct((rows.shape...]
  transfers between devices with their start and end apart: 37 -> 6, of which waited for: 5 -> 4; matrix products, arithmetic and copies ran while one was open for 65% -> 1% of each run, Pallas kernels for 0% -> 0%
where the time goes in v1:
time: 442 us; the launch traced here: 441 us
  waiting for transfers between devices  351 us (79%)
  Pallas kernels  34.4 us (8%)
  blocking collectives  29.1 us (7%)
  between operations  16.1 us (4%)
    all_gather x1, waiting for transfers between devices, on_device(): column_rows = lax.all_gather(got, 'row', axis=0, tiled=True)  227 us
    ppermute x3, waiting for transfers between devices, on_device(): lax.ppermute(s_own, 'row', [(i, (i + d) % rows_n) for i in range(rows_n)])  87 us
    all_gather x1, waiting for transfers between devices, on_device(): p_all = lax.all_gather(dense, 'col', axis=0, tiled=True)  36.2 us
    pallas_call x1, Pallas kernels, density_blocks(): pl.pallas_call(density_kernel, out_shape=jax.ShapeDtypeStruct((rows.shape...  18 us
    pallas_call x1, Pallas kernels, product_blocks(): pl.pallas_call(product_kernel, out_shape=jax.ShapeDtypeStruct((counts.sha...  16.4 us
    all_gather x1, blocking collectives, on_device(): p_codes = lax.all_gather(p_code, 'col').reshape(-1)  15 us
    all_gather x1, blocking collectives, on_device(): s_codes = lax.all_gather(s_code, 'row').reshape(-1)  14.2 us
  transfers between devices with their start and end apart: 6, of which 4 were waited for; matrix products, arithmetic and copies ran while one was open for 1% of the time, Pallas kernels for 0%

profile of v1, /device:TPU:0, one launch (start us, length us, event | category | flops | bytes accessed | tf_op | source)
XLA Modules:
  0.0 441.5 jit_solution(15747731558685975285)
XLA Ops:
  7.2 1.7 constant_dynamic-slice_fusion
  9.0 0.8 collective-permute-start
  9.8 1.3 copy-done
  11.8 0.5 and_select_fusion.9
  12.4 227.4 %all-gather.5.cloned.1.call-done = bf16[2048,2048]{1,0:T(8,128)(2,1)} async-done(((bf16[512,2048]{1,0:T(8,128)(2,1)}), bf16[2048,2048]{1,0:T(8,128)(2,1)}) %all-gather.5.cloned.1.call-update) | async-done | bytes 8388624 | tf_op jit(solution)/shard_map/all_gather | solution.py:142
  239.8 18.0 %density_blocks.1 = bf16[64,128,128]{2,1,0:T(8,128)(2,1)} custom-call(s32[1]{0:T(128)} %bitcast.49.count_ref, s32[64]{0:T(128)} %get-tuple-element.24.row_ref, s32[64]{0:T(128)} %get-tuple-element.23.col_ref, bf16[32,128,2048]{2,1,0:T(8,128)(2,1)} %bitcast.53, bf16[16,128,2048]{2,1,0:T(8,128)(2,1)} %bitcast.54), custom_call_target="tpu_custom_call" | custom-call | tf_op jit(solution)/shard_map/density_blocks/pallas_call | solution.py:34
  258.5 14.2 %all-gather.1 = s32[4,1,64]{2,1,0:T(1,128)S(1)} all-gather(s32[1,1,64]{2,1,0:T(1,128)S(1)} %fusion.38), channel_id=1, replica_groups=mesh['row'=4,'col'=8] {'row'}, dimensions={0}, use_global_device_ids=true | all-gather | bytes 1280 | tf_op jit(solution)/shard_map/all_gather | solution.py:157
  272.7 15.0 %all-gather = s32[8,1,64]{2,1,0:T(1,128)S(1)} all-gather(s32[1,1,64]{2,1,0:T(1,128)S(1)} %fusion.37), channel_id=1, replica_groups=mesh['row'=4,'col'=8] {'col'}, dimensions={0}, use_global_device_ids=true | all-gather | bytes 2304 | tf_op jit(solution)/shard_map/all_gather | solution.py:156
  287.7 1.6 collective-permute-start.3
  289.3 0.3 collective-permute-start.2
  289.6 0.6 collective-permute-start.1
  290.8 0.1 ge.23
  290.9 0.1 ne.279
  291.2 0.1 ge.21
  291.2 0.1 ne.267
  291.6 0.3 fusion.1
  291.9 1.0 convert_reduce_fusion
  292.9 0.1 convolution_convert_fusion
  293.0 1.3 select_reduce_fusion
  294.3 0.7 add_select_fusion
  295.0 41.4 %collective-permute-done.3.rest_3_ = bf16[64,128,128]{2,1,0:T(8,128)(2,1)} collective-permute-done((bf16[64,128,128]{2,1,0:T(8,128)(2,1)S(1)}, bf16[64,128,128]{2,1,0:T(8,128)(2,1)}, u32[]{:S(2)}, u32[]{:S(2)}) %collective-permute-start.3) | collective-permute-done | bytes 2097184 | tf_op jit(solution)/shard_map/ppermute | solution.py:192
  336.4 45.6 %collective-permute-done.2.rest_2_ = bf16[64,128,128]{2,1,0:T(8,128)(2,1)} collective-permute-done((bf16[64,128,128]{2,1,0:T(8,128)(2,1)S(1)}, bf16[64,128,128]{2,1,0:T(8,128)(2,1)}, u32[]{:S(2)}, u32[]{:S(2)}) %collective-permute-start.2) | collective-permute-done | bytes 2097184 | tf_op jit(solution)/shard_map/ppermute | solution.py:192
  382.0 36.2 %all-gather.7.cloned.1.call-done.p_hbm = bf16[512,128,128]{2,1,0:T(8,128)(2,1)} async-done(((bf16[64,128,128]{2,1,0:T(8,128)(2,1)}), bf16[512,128,128]{2,1,0:T(8,128)(2,1)}) %all-gather.7.cloned.1.call-update) | async-done | bytes 16777232 | tf_op jit(solution)/shard_map/all_gather | solution.py:188
  418.2 16.4 %product_blocks.1 = f32[64,128,128]{2,1,0:T(8,128)} custom-call(s32[64]{0:T(128)} %get-tuple-element.12.count_ref, s32[64,128]{1,0:T(8,128)} %get-tuple-element.16.left_at, s32[64,128]{1,0:T(8,128)} %get-tuple-element.15.right_at, bf16[512,128,128]{2,1,0:T(8,128)(2,1)} %all-gather.7.cloned.1.call-done.p_hbm, bf16[64,128,128]{2,1,0:T(8,128)(2,1)} %bitcast.57, ...), custom_call_target="tpu_custom_call" | custom-call | tf_op jit(solution)/shard_map/product_blocks/pallas_call | solution.py:91
  (30 shorter events, 0.6 us)
Async XLA Ops:
  7.2 4.7 %copy-start.3 = (s32[1,1,64]{2,1,0:T(1,128)S(1)}, s32[1,1,64]{2,1,0:T(1,128)}, u32[]{:S(2)}) copy-start(s32[1,1,64]{2,1,0:T(1,128)} %param.9) | copy-start | bytes 772
  7.2 232.6 %all-gather.5.cloned.1.call-start = ((), (), s32[]{:S(2)}) async-start(), calls=%async_computation | async-start | bytes 10485760 | tf_op jit(solution)/shard_map/all_gather | solution.py:142
  9.0 0.8 collective-permute-start
  9.8 1.3 copy-start
  11.1 407.1 %all-gather.7.cloned.1.call-start = ((), (), s32[]{:S(2)}) async-start(), calls=%async_computation.1 | async-start | bytes 18874368 | tf_op jit(solution)/shard_map/all_gather | solution.py:188
  239.8 18.7 %copy-start.2 = (s32[1,1,64]{2,1,0:T(1,128)S(1)}, s32[1,1,64]{2,1,0:T(1,128)}, u32[]{:S(2)}) copy-start(s32[1,1,64]{2,1,0:T(1,128)} %param.12) | copy-start | bytes 772
  239.8 47.9 %copy-start.1 = (bf16[1,1,64,128,128]{4,3,2,1,0:T(8,128)(2,1)S(1)}, bf16[1,1,64,128,128]{4,3,2,1,0:T(8,128)(2,1)}, u32[]{:S(2)}) copy-start(bf16[1,1,64,128,128]{4,3,2,1,0:T(8,128)(2,1)} %param.11) | copy-start | bytes 6291460
  239.8 51.7 %copy-start.4 = (s32[1,1,64]{2,1,0:T(1,128)S(1)}, s32[1,1,64]{2,1,0:T(1,128)}, u32[]{:S(2)}) copy-start(s32[1,1,64]{2,1,0:T(1,128)} %param.14) | copy-start | bytes 772
  287.7 48.7 %collective-permute-start.3 = (bf16[64,128,128]{2,1,0:T(8,128)(2,1)S(1)}, bf16[64,128,128]{2,1,0:T(8,128)(2,1)}, u32[]{:S(2)}, u32[]{:S(2)}) collective-permute-start(bf16[64,128,128]{2,1,0:T(8,128)(2,1)S(1)} %bitcast.58), channel_id=1, source_target_pairs={{0,24},{8,0},{16,8},{24,16},{1,25},{9,1},{17,9},{25,17},{2,26},{10... | collective-permute-start | bytes 6291464 | tf_op jit(solution)/shard_map/ppermute | solution.py:192
  289.3 92.7 %collective-permute-start.2 = (bf16[64,128,128]{2,1,0:T(8,128)(2,1)S(1)}, bf16[64,128,128]{2,1,0:T(8,128)(2,1)}, u32[]{:S(2)}, u32[]{:S(2)}) collective-permute-start(bf16[64,128,128]{2,1,0:T(8,128)(2,1)S(1)} %bitcast.59), channel_id=1, source_target_pairs={{0,16},{8,24},{16,0},{24,8},{1,17},{9,25},{17,1},{25,9},{2,18},{10... | collective-permute-start | bytes 6291464 | tf_op jit(solution)/shard_map/ppermute | solution.py:192
  289.6 92.4 %collective-permute-start.1 = (bf16[64,128,128]{2,1,0:T(8,128)(2,1)S(1)}, bf16[64,128,128]{2,1,0:T(8,128)(2,1)}, u32[]{:S(2)}, u32[]{:S(2)}) collective-permute-start(bf16[64,128,128]{2,1,0:T(8,128)(2,1)S(1)} %bitcast.60), channel_id=1, source_target_pairs={{0,8},{8,16},{16,24},{24,0},{1,9},{9,17},{17,25},{25,1},{2,10},{10... | collective-permute-start | bytes 6291464 | tf_op jit(solution)/shard_map/ppermute | solution.py:192
Sparse Core Ops, SparseCore 0:
  11.3 228.4 all-gather.4
  258.0 160.2 all-gather.6
